TPU v7x, 128 devices: a whole 4x4x4 slice. The times are simulated.
128 devices in a mesh: dp: 2 (over core), ctx: 64 (over z, x, y).
Axes of the slice: x: 4, y: 4, z: 4, core: 2. Of those that a mesh axis runs over, the one named last changes fastest.
Arguments:
- tokens: bfloat16 [32768, 4096], P(('dp', 'ctx')), parts along dimension 0, may hold values from -6 to 19
- positions: int32 [32768], P('dp'), parts along dimension 0, may hold values from 0 to 16383, as said below
- lengths: int32 [256], P('dp'), parts along dimension 0, may hold values from 1 to 384, 16384 in all
- gain: bfloat16 [4096], replicated, may hold values from 0.5 to 1.5
- w_query: bfloat16 [4096, 2048], replicated, may hold values from -0.09375 to 0.09375
- w_key: bfloat16 [4096, 512], replicated, may hold values from -0.09375 to 0.09375
- value_weight: bfloat16 [4096, 512], replicated, may hold values from -0.09375 to 0.09375
Outputs:
- attended: bfloat16 [32768, 2048], P(('dp', 'ctx')), parts along dimension 0
There are 2 independent parts, one for each index of `dp`. A program takes and returns all parts, laid end to end along the dimension named above; an argument that names none is the same for every part. Nothing has to cross between parts.
Inputs may be any that keep to these rules, and one draw needn't show every extreme that they name: positions is a permutation; every aligned block of 256 rows holds exactly 4 positions of each owner j, whose positions are j * 128 to j * 128 + 127 and (2 * 64 - 1 - j) * 128 to (2 * 64 - j) * 128 - 1.
All inputs are finite; a program needn't handle non-finite values.
Results may differ from a plain program's by a relative error of at most 0.012.
The roundings to bfloat16 on the way count: a program that leaves them out, or rounds other values in their place, can miss the bound.
Values may be sent and summed in bfloat16 or wider, within the bound.
A program may use at most 128 MiB of HBM per device.

v0:
```python
import jax
import jax.numpy as jnp
from jax import lax
from jax.sharding import PartitionSpec as P

HEAD_SIZE = 128


ROPE_THETA = 500000.0
EPSILON = 1e-05


def from_behind(block, axis, distance):
    devices = range(lax.axis_size(axis))
    route = [(i - distance, i) for i in devices if i - distance in devices]
    return lax.ppermute(block, axis, route)


def rope(values, where_at):
    heads = values.shape[1] // HEAD_SIZE
    half = HEAD_SIZE // 2
    shaped = values.reshape(values.shape[0], heads, HEAD_SIZE)
    freq = ROPE_THETA ** (-(jnp.arange(half, dtype=jnp.float32) * 2.0 / HEAD_SIZE))
    angle = where_at.astype(jnp.float32)[:, None, None] * freq[None, None, :]
    cosine = jnp.cos(angle)
    sine = jnp.sin(angle)
    first = shaped[..., :half]
    second = shaped[..., half:]
    turned = jnp.concatenate(
        [first * cosine - second * sine, second * cosine + first * sine], axis=-1
    )
    return turned.reshape(values.shape[0], heads * HEAD_SIZE)


def project(tokens, gain, w_query, w_key, value_weight, where_at):
    floats = tokens.astype(jnp.float32)
    score_scale = lax.rsqrt(jnp.mean(floats * floats, axis=-1, keepdims=True) + EPSILON)
    normed = (floats * score_scale * gain.astype(jnp.float32)).astype(jnp.bfloat16)
    query = rope(jnp.dot(normed, w_query, preferred_element_type=jnp.float32), where_at).astype(
        jnp.bfloat16
    )
    key = rope(jnp.dot(normed, w_key, preferred_element_type=jnp.float32), where_at).astype(
        jnp.bfloat16
    )
    value = jnp.dot(normed, value_weight, preferred_element_type=jnp.float32).astype(jnp.bfloat16)
    return (query, key, value)


def doc_of(where_at, lengths):
    ends = jnp.cumsum(lengths, dtype=jnp.int32)
    return jnp.sum((ends[None, :] <= where_at[:, None]).astype(jnp.int32), axis=1)


def attend(query, key, value, query_at, key_at, key_valid, lengths):
    rows = query.shape[0]
    keys = key.shape[0]
    kv_heads = key.shape[1] // HEAD_SIZE
    group = query.shape[1] // HEAD_SIZE // kv_heads
    query_doc = doc_of(query_at, lengths)
    key_doc = doc_of(key_at, lengths)
    allowed = (
        (key_doc[None, :] == query_doc[:, None])
        & (key_at[None, :] <= query_at[:, None])
        & key_valid[None, :]
    )
    q_heads = query.reshape(rows, kv_heads, group, HEAD_SIZE)
    k_heads = key.reshape(keys, kv_heads, HEAD_SIZE)
    v_heads = value.reshape(keys, kv_heads, HEAD_SIZE)
    scores = jnp.einsum("rhgd,khd->hgrk", q_heads, k_heads, preferred_element_type=jnp.float32) * (
        1.0 / HEAD_SIZE**0.5
    )
    scores = jnp.where(allowed[None, None], scores, jnp.float32(-1e30))
    top = jnp.max(scores, axis=-1, keepdims=True)
    weights = jnp.exp(scores - top)
    total = jnp.sum(weights, axis=-1)
    rounded = weights.astype(jnp.bfloat16)
    mixed = jnp.einsum("hgrk,khd->rhgd", rounded, v_heads, preferred_element_type=jnp.float32)
    mixed = mixed / jnp.transpose(total, (2, 0, 1))[..., None]
    return mixed.reshape(rows, kv_heads * group * HEAD_SIZE).astype(jnp.bfloat16)


def zig_positions(owner, rows, cycle_size):
    inner = jnp.arange(rows, dtype=jnp.int32)
    half_rows = rows // 2
    return jnp.where(
        inner < half_rows,
        owner * half_rows + inner,
        (2 * cycle_size - 1 - owner) * half_rows + inner - half_rows,
    )


def inside(source, count, cycle_size):
    return jnp.broadcast_to((source >= 0) & (source < cycle_size), (count,))


def attend_pieces(query, query_at, pieces, key_at, key_valid, lengths, kv_width):
    all_kv = jnp.concatenate(pieces, axis=0)
    where_keys = jnp.concatenate(key_at, axis=0)
    valid_keys = jnp.concatenate(key_valid, axis=0)
    return attend(
        query, all_kv[:, :kv_width], all_kv[:, kv_width:], query_at, where_keys, valid_keys, lengths
    )


def shards(tokens, positions, lengths, gain, w_query, w_key, value_weight):
    cycle_size = lax.axis_size("ctx")
    device = lax.axis_index("ctx")
    rows = tokens.shape[0]
    half_rows = rows // 2
    per_peer = rows // cycle_size
    total_rows = rows * cycle_size

    def owner_of(where_at):
        block_id = where_at // half_rows
        return jnp.minimum(block_id, 2 * cycle_size - 1 - block_id)

    mine = lax.dynamic_slice_in_dim(positions, device * rows, rows, 0)
    send_order = jnp.argsort(owner_of(mine) * total_rows + mine)
    table = positions.reshape(cycle_size, rows)
    marked = jnp.where(owner_of(table) == device, table, total_rows)
    arrived = jnp.sort(marked, axis=1)[:, :per_peer].reshape(rows)
    slot_of = jnp.where(
        arrived // half_rows == device,
        arrived - device * half_rows,
        arrived - (2 * cycle_size - 1 - device) * half_rows + half_rows,
    )
    placing = jnp.argsort(slot_of)
    local_at = zig_positions(device, rows, cycle_size)
    kv_width = w_key.shape[1]
    outgoing = tokens[send_order].reshape(cycle_size, per_peer, tokens.shape[1])
    received = lax.all_to_all(outgoing, "ctx", split_axis=0, concat_axis=0, tiled=True).reshape(
        rows, tokens.shape[1]
    )[placing]
    query, key, value = project(received, gain, w_query, w_key, value_weight, local_at)
    kv_local = jnp.concatenate([key, value], axis=1)
    pieces = [kv_local]
    sources = [device]
    for offset in (1, 2, 3, -1, -2, -3):
        pieces.append(from_behind(kv_local, "ctx", offset))
        sources.append(device - offset)
    attended = attend_pieces(
        query,
        local_at,
        pieces,
        [zig_positions(source, rows, cycle_size) for source in sources],
        [inside(source, rows, cycle_size) for source in sources],
        lengths,
        kv_width,
    )
    return attended


def solution(mesh):
    in_specs = (P(("dp", "ctx"), None), P("dp"), P("dp"), P(), P(), P(), P())
    out_specs = P(("dp", "ctx"), None)
    return jax.shard_map(shards, mesh=mesh, in_specs=in_specs, out_specs=out_specs, check_vma=False)
```

profile of v0, /device:TPU:0, one launch (start us, length us, event | category | flops | bytes accessed | tf_op | source)
XLA Modules:
  0.0 197.8 jit_solution(7243801550734352166)
XLA Ops:
  6.5 0.0 copy-start
  6.5 1.0 reshape.227
  7.6 0.7 fusion.17
  8.2 0.0 sort.43.cloned.1.call-update
  8.3 0.8 fusion.19
  9.0 3.2 %sort.39 = (s32[256]{0:T(256)}, s32[256]{0:T(256)S(1)}) sort(s32[256]{0:T(256)S(1)} %fusion.19, s32[256]{0:T(256)S(1)} %iota.67), dimensions={0}, to_apply=%region_0.1 | sort | flops 2048 | bytes 4096 | tf_op jit(solution)/shard_map/jit(argsort)/sort | solution.py:118
  12.3 3.1 %gather_fusion = bf16[256,4096]{1,0:T(8,128)(2,1)} fusion(bf16[256,4096]{1,0:T(8,128)(2,1)S(1)} %copy-done, s32[1024]{0:T(1024)S(1)} %pad_clamp_fusion.1), kind=kCustom, calls=%fused_computation | custom fusion | bytes 4195328 | tf_op jit(solution)/shard_map/gather | solution.py:130
  15.4 4.1 %reshape.225 = bf16[64,4,4096]{2,1,0:T(4,128)(2,1)} reshape(bf16[256,4096]{1,0:T(8,128)(2,1)} %gather_fusion) | data formatting | bytes 4194304 | tf_op jit(solution)/shard_map/reshape | solution.py:130
  19.5 12.0 %all-to-all-start = ((bf16[64,4,4096]{2,1,0:T(4,128)(2,1)}), bf16[64,4,4096]{2,1,0:T(4,128)(2,1)}, u32[]{:S(2)}, u32[]{:S(2)}) async-start(bf16[64,4,4096]{2,1,0:T(4,128)(2,1)} %reshape.225), calls=%async_computation | async-start | bytes 4194304 | tf_op jit(solution)/shard_map/all_to_all | solution.py:131
  31.5 0.1 copy.20
  31.7 0.2 reduce-window.8
  31.8 0.1 reduce
  32.0 0.5 multiply_cosine_fusion
  32.5 0.2 convert_reduce_fusion.1
  32.8 0.3 dynamic-update-slice
  33.1 0.2 dynamic-update-slice.1
  33.3 0.2 dynamic-update-slice.2
  33.5 0.2 dynamic-update-slice.3
  33.8 0.2 dynamic-update-slice.4
  34.0 0.2 dynamic-update-slice.5
  34.3 0.2 dynamic-update-slice.6
  34.5 0.8 slice.32
  35.2 0.1 reshape.228
  35.4 3.2 %sort.41 = (s32[256]{0:T(256)}, s32[256]{0:T(256)S(1)}) sort(s32[256]{0:T(256)S(1)} %get-tuple-element.22, s32[256]{0:T(256)S(1)} %iota.68), dimensions={0}, to_apply=%region_2.3 | sort | flops 2048 | bytes 4096 | tf_op jit(solution)/shard_map/jit(argsort)/sort | solution.py:127
  38.7 0.6 convert_reduce_fusion
  39.2 1.6 and_and_fusion
  40.9 19.9 %all-to-all-done = bf16[64,4,4096]{2,1,0:T(4,128)(2,1)} async-done(((bf16[64,4,4096]{2,1,0:T(4,128)(2,1)}), bf16[64,4,4096]{2,1,0:T(4,128)(2,1)}, u32[]{:S(2)}, u32[]{:S(2)}) %all-to-all-start) | async-done | bytes 2097184 | tf_op jit(solution)/shard_map/all_to_all | solution.py:131
  60.8 2.5 %reshape.226 = bf16[256,4096]{1,0:T(8,128)(2,1)S(1)} reshape(bf16[64,4,4096]{2,1,0:T(4,128)(2,1)} %all-to-all-done) | data formatting | bytes 4194304 | tf_op jit(solution)/shard_map/reshape | solution.py:131
  63.3 3.2 %gather_fusion.1 = bf16[256,4096]{1,0:T(8,128)(2,1)} fusion(bf16[256,4096]{1,0:T(8,128)(2,1)S(1)} %reshape.226, s32[1024]{0:T(1024)S(1)} %pad_clamp_fusion), kind=kCustom, calls=%fused_computation.1 | custom fusion | bytes 4195328 | tf_op jit(solution)/shard_map/gather | solution.py:131
  66.5 2.1 %fusion.6 = f32[256]{0:T(256)S(1)} fusion(bf16[256,4096]{1,0:T(8,128)(2,1)} %gather_fusion.1), kind=kLoop, calls=%fused_computation.11 | loop fusion | flops 3145472 | bytes 2098176 | tf_op jit(solution)/shard_map/reduce_sum | solution.py:37
  68.6 0.0 copy-start.6
  68.6 5.0 %convolution_convert_fusion = bf16[256,512]{1,0:T(8,128)(2,1)} fusion(bf16[4096,512]{1,0:T(8,128)(2,1)} %param.13, bf16[256,4096]{1,0:T(8,128)(2,1)} %gather_fusion.1, f32[4096]{0:T(1024)S(1)} %convert_element_type.45, f32[256]{0:T(256)S(1)} %add_rsqrt_fusion), kind=kOutput, calls=%fused_computation.22 | convolution fusion | flops 1078067200 | bytes 6571008 | tf_op jit(solution)/shard_map/dot_general | solution.py:45
  73.6 0.0 copy-done.2
  73.6 2.1 %fusion.25 = f32[256,512]{1,0:T(8,128)} fusion(bf16[4096,512]{1,0:T(8,128)(2,1)S(1)} %copy-done.6, bf16[256,4096]{1,0:T(8,128)(2,1)S(1)} %copy-done.2, f32[4096]{0:T(1024)S(1)} %convert_element_type.45, f32[256]{0:T(256)S(1)} %add_rsqrt_fusion), kind=kOutput, calls=%fused_computation.80 | convolution fusion | flops 1077936128 | bytes 6833152 | tf_op jit(solution)/shard_map/dot_general | solution.py:42
  75.7 1.2 reshape.229
  76.9 0.5 subtract_convert_fusion.1
  77.4 0.4 pad_maximum_fusion.2
  77.8 1.1 pad_maximum_fusion.1
  78.9 1.3 collective-permute-start.4
  80.2 1.3 collective-permute-start.3
  81.5 7.3 %collective-permute-start.2 = (bf16[256,1024]{1,0:T(8,128)(2,1)S(1)}, bf16[256,1024]{1,0:T(8,128)(2,1)S(1)}, u32[]{:S(2)}, u32[]{:S(2)}) collective-permute-start(bf16[256,1024]{1,0:T(8,128)(2,1)S(1)} %get-tuple-element.15), channel_id=1, source_target_pairs={{0,3},{1,4},{2,5},{3,6},{4,7},{5,8},{6,9},{7,10},{8,11},{9,12},{10... | collective-permute-start | bytes 1572872 | tf_op jit(solution)/shard_map/ppermute | solution.py:16
  88.8 4.6 %collective-permute-start.1 = (bf16[256,1024]{1,0:T(8,128)(2,1)S(1)}, bf16[256,1024]{1,0:T(8,128)(2,1)S(1)}, u32[]{:S(2)}, u32[]{:S(2)}) collective-permute-start(bf16[256,1024]{1,0:T(8,128)(2,1)S(1)} %get-tuple-element.15), channel_id=1, source_target_pairs={{0,2},{1,3},{2,4},{3,5},{4,6},{5,7},{6,8},{7,9},{8,10},{9,11},{10,... | collective-permute-start | bytes 1572872 | tf_op jit(solution)/shard_map/ppermute | solution.py:16
  93.4 1.5 collective-permute-start
  95.0 8.2 %convolution_bitcast_fusion = f32[32,8,16,128]{3,1,2,0:T(8,128)S(1)} fusion(bf16[4096,2048]{1,0:T(8,128)(2,1)} %param.11, bf16[256,4096]{1,0:T(8,128)(2,1)S(1)} %copy-done.2, f32[4096]{0:T(1024)S(1)} %convert_element_type.45, f32[256]{0:T(256)S(1)} %add_rsqrt_fusion), kind=kOutput, calls=%fused_computation.21 | convolution fusion | flops 4299161600 | bytes 20988928 | tf_op jit(solution)/shard_map/dot_general | solution.py:39
  103.2 0.4 copy.33
  103.6 0.8 subtract_convert_fusion
  104.3 0.6 pad_maximum_fusion
  104.9 1.2 copy.21
  106.2 9.0 %collective-permute-done = bf16[256,1024]{1,0:T(8,128)(2,1)S(1)} collective-permute-done((bf16[256,1024]{1,0:T(8,128)(2,1)S(1)}, bf16[256,1024]{1,0:T(8,128)(2,1)S(1)}, u32[]{:S(2)}, u32[]{:S(2)}) %collective-permute-start) | collective-permute-done | bytes 524320 | tf_op jit(solution)/shard_map/ppermute | solution.py:16
  115.2 1.3 collective-permute-start.5
  116.5 0.0 collective-permute-done.1
  116.6 0.0 collective-permute-done.2
  116.7 0.0 collective-permute-done.3
  116.7 0.0 collective-permute-done.4
  116.8 22.7 %collective-permute-done.5 = bf16[256,1024]{1,0:T(8,128)(2,1)S(1)} collective-permute-done((bf16[256,1024]{1,0:T(8,128)(2,1)S(1)}, bf16[256,1024]{1,0:T(8,128)(2,1)S(1)}, u32[]{:S(2)}, u32[]{:S(2)}) %collective-permute-start.5) | collective-permute-done | bytes 524320 | tf_op jit(solution)/shard_map/ppermute | solution.py:16
  139.5 1.5 fusion.27
  141.0 4.2 %reshape.233 = bf16[1792,4,128]{2,1,0:T(4,128)(2,1)} reshape(bf16[1792,512]{1,0:T(8,128)(2,1)} %get-tuple-element.9) | data formatting | bytes 3670016 | tf_op jit(solution)/shard_map/reshape | solution.py:67
  145.2 2.5 %copy.29 = bf16[1792,512]{0,1:T(8,128)(2,1)} copy(bf16[1792,512]{1,0:T(8,128)(2,1)S(1)} %get-tuple-element.10) | data formatting | bytes 3670016 | tf_op jit(solution)/shard_map/reshape | solution.py:68
  147.7 13.6 %fusion.2 = (f32[4,4,256]{2,1,0:T(4,128)S(1)}, f32[4,1792,256,4]{2,1,3,0:T(8,128)}) fusion(pred[256,1792]{0,1:T(8,128)(4,1)S(1)} %and_and_fusion, bf16[256,4,4,128]{3,0,2,1:T(8,128)(2,1)} %bitcast.39, bf16[1792,4,128,1]{2,1,0,3:T(4,128)(2,1)} %bitcast.38), kind=kOutput, calls=%fused_computation.6 | convolution fusion | flops 1901064192 | bytes 32718848 | tf_op jit(solution)/shard_map/rhgd,khd->hgrk/dot_general | solution.py:69
  161.3 12.8 %fusion = f32[4,4,256]{2,1,0:T(4,128)S(1)} fusion(f32[4,1792,256,4]{2,1,3,0:T(8,128)} %get-tuple-element.20, f32[4,4,256]{2,1,0:T(4,128)S(1)} %get-tuple-element.19, pred[256,1792]{0,1:T(8,128)(4,1)S(1)} %and_and_fusion), kind=kLoop, calls=%fused_computation.4 | loop fusion | flops 29356032 | bytes 29851648 | tf_op jit(solution)/shard_map/reduce_sum | solution.py:75
  174.1 0.0 copy-done.3
  174.1 0.0 copy-start.1
  174.2 14.5 %fusion.9 = bf16[256,4,4,128]{0,3,2,1:T(8,128)(2,1)} fusion(bf16[1792,4,128,1]{0,2,3,1:T(8,128)(2,1)S(1)} %bitcast.40, f32[4,1792,256,4]{2,1,3,0:T(8,128)} %get-tuple-element.20, f32[4,4,256]{2,1,0:T(4,128)S(1)} %get-tuple-element.19, pred[256,1792]{0,1:T(8,128)(4,1)S(1)} %and_and_fusion, f32[256,4,4]{0,2,1:T(4,128)S(1)} %bitcast.44), kind=kOutput, calls=%fused_computation.15 | convolution fusion | flops 1909456896 | bytes 32735232 | tf_op jit(solution)/shard_map/hgrk,khd->rhgd/dot_general | solution.py:77
  188.7 2.3 %copy.25 = bf16[256,2048]{1,0:T(8,128)(2,1)} copy(bf16[256,2048]{0,1:T(8,128)(2,1)} %bitcast.42) | data formatting | bytes 2097152 | tf_op jit(solution)/shard_map/convert_element_type | solution.py:79
  (44 shorter events, 0.4 us)
Async XLA Ops:
  6.5 5.7 %copy-start = (bf16[256,4096]{1,0:T(8,128)(2,1)S(1)}, bf16[256,4096]{1,0:T(8,128)(2,1)}, u32[]{:S(2)}) copy-start(bf16[256,4096]{1,0:T(8,128)(2,1)} %param.7) | copy-start | bytes 6291460
  6.5 27.9 %sort.43.cloned.1.call-start = ((), (), s32[]{:S(2)}) async-start(), calls=%async_computation.1 | async-start | bytes 196640 | tf_op jit(solution)/shard_map/jit(sort)/sort | solution.py:121
  15.4 16.1 %copy-start.5 = (s32[128]{0:T(128)S(1)}, s32[128]{0:T(128)}, u32[]{:S(2)}) copy-start(s32[128]{0:T(128)} %param.9) | copy-start | bytes 1540
  15.4 17.3 %copy-start.4 = (bf16[4096]{0:T(1024)(128)(2,1)S(1)}, bf16[4096]{0:T(1024)(128)(2,1)}, u32[]{:S(2)}) copy-start(bf16[4096]{0:T(1024)(128)(2,1)} %param.10) | copy-start | bytes 24580
  19.5 41.2 %all-to-all-start = ((bf16[64,4,4096]{2,1,0:T(4,128)(2,1)}), bf16[64,4,4096]{2,1,0:T(4,128)(2,1)}, u32[]{:S(2)}, u32[]{:S(2)}) async-start(bf16[64,4,4096]{2,1,0:T(4,128)(2,1)} %reshape.225), calls=%async_computation | async-start | bytes 4194304 | tf_op jit(solution)/shard_map/all_to_all | solution.py:131
  68.6 5.0 %copy-start.2 = (bf16[256,4096]{1,0:T(8,128)(2,1)S(1)}, bf16[256,4096]{1,0:T(8,128)(2,1)}, u32[]{:S(2)}) copy-start(bf16[256,4096]{1,0:T(8,128)(2,1)} %gather_fusion.1) | copy-start | bytes 6291460
  68.6 5.0 %copy-start.6 = (bf16[4096,512]{1,0:T(8,128)(2,1)S(1)}, bf16[4096,512]{1,0:T(8,128)(2,1)}, u32[]{:S(2)}) copy-start(bf16[4096,512]{1,0:T(8,128)(2,1)} %param.12) | copy-start | bytes 12582916
  78.9 37.8 %collective-permute-start.4 = (bf16[256,1024]{1,0:T(8,128)(2,1)S(1)}, bf16[256,1024]{1,0:T(8,128)(2,1)S(1)}, u32[]{:S(2)}, u32[]{:S(2)}) collective-permute-start(bf16[256,1024]{1,0:T(8,128)(2,1)S(1)} %get-tuple-element.15), channel_id=1, source_target_pairs={{2,0},{3,1},{4,2},{5,3},{6,4},{7,5},{8,6},{9,7},{10,8},{11,9},{12,... | collective-permute-start | bytes 1572872 | tf_op jit(solution)/shard_map/ppermute | solution.py:16
  80.2 36.4 %collective-permute-start.3 = (bf16[256,1024]{1,0:T(8,128)(2,1)S(1)}, bf16[256,1024]{1,0:T(8,128)(2,1)S(1)}, u32[]{:S(2)}, u32[]{:S(2)}) collective-permute-start(bf16[256,1024]{1,0:T(8,128)(2,1)S(1)} %get-tuple-element.15), channel_id=1, source_target_pairs={{1,0},{2,1},{3,2},{4,3},{5,4},{6,5},{7,6},{8,7},{9,8},{10,9},{11,1... | collective-permute-start | bytes 1572872 | tf_op jit(solution)/shard_map/ppermute | solution.py:16
  81.5 35.1 %collective-permute-start.2 = (bf16[256,1024]{1,0:T(8,128)(2,1)S(1)}, bf16[256,1024]{1,0:T(8,128)(2,1)S(1)}, u32[]{:S(2)}, u32[]{:S(2)}) collective-permute-start(bf16[256,1024]{1,0:T(8,128)(2,1)S(1)} %get-tuple-element.15), channel_id=1, source_target_pairs={{0,3},{1,4},{2,5},{3,6},{4,7},{5,8},{6,9},{7,10},{8,11},{9,12},{10... | collective-permute-start | bytes 1572872 | tf_op jit(solution)/shard_map/ppermute | solution.py:16
  88.8 27.8 %collective-permute-start.1 = (bf16[256,1024]{1,0:T(8,128)(2,1)S(1)}, bf16[256,1024]{1,0:T(8,128)(2,1)S(1)}, u32[]{:S(2)}, u32[]{:S(2)}) collective-permute-start(bf16[256,1024]{1,0:T(8,128)(2,1)S(1)} %get-tuple-element.15), channel_id=1, source_target_pairs={{0,2},{1,3},{2,4},{3,5},{4,6},{5,7},{6,8},{7,9},{8,10},{9,11},{10,... | collective-permute-start | bytes 1572872 | tf_op jit(solution)/shard_map/ppermute | solution.py:16
  93.4 21.8 %collective-permute-start = (bf16[256,1024]{1,0:T(8,128)(2,1)S(1)}, bf16[256,1024]{1,0:T(8,128)(2,1)S(1)}, u32[]{:S(2)}, u32[]{:S(2)}) collective-permute-start(bf16[256,1024]{1,0:T(8,128)(2,1)S(1)} %get-tuple-element.15), channel_id=1, source_target_pairs={{0,1},{1,2},{2,3},{3,4},{4,5},{5,6},{6,7},{7,8},{8,9},{9,10},{10,1... | collective-permute-start | bytes 1572872 | tf_op jit(solution)/shard_map/ppermute | solution.py:16
  115.2 24.2 %collective-permute-start.5 = (bf16[256,1024]{1,0:T(8,128)(2,1)S(1)}, bf16[256,1024]{1,0:T(8,128)(2,1)S(1)}, u32[]{:S(2)}, u32[]{:S(2)}) collective-permute-start(bf16[256,1024]{1,0:T(8,128)(2,1)S(1)} %get-tuple-element.15), channel_id=1, source_target_pairs={{3,0},{4,1},{5,2},{6,3},{7,4},{8,5},{9,6},{10,7},{11,8},{12,9},{13... | collective-permute-start | bytes 1572872 | tf_op jit(solution)/shard_map/ppermute | solution.py:16
  161.3 12.8 %copy-start.3 = (bf16[1792,512]{0,1:T(8,128)(2,1)S(1)}, bf16[1792,512]{0,1:T(8,128)(2,1)}, u32[]{:S(2)}) copy-start(bf16[1792,512]{0,1:T(8,128)(2,1)} %copy.29) | copy-start | bytes 5505028
  174.1 16.8 %copy-start.1 = (bf16[256,4096]{1,0:T(8,128)(2,1)S(1)}, bf16[256,4096]{1,0:T(8,128)(2,1)}, u32[]{:S(2)}) copy-start(bf16[256,4096]{1,0:T(8,128)(2,1)} %param.7) | copy-start | bytes 6291460
Sparse Core Ops, SparseCore 0:
  9.6 4.6 sort.45.cloned.1.call-done
  (1 shorter events, 0.0 us)
where the time goes:
time: 200 us; the launch traced here: 198 us
  waiting for transfers between devices  51.6 us (26%)
  matrix products  43.4 us (22%)
  local copies, waits for them, and re-layouts  30.3 us (15%)
  other arithmetic  29.3 us (15%)
  starting transfers between devices  29.3 us (15%)
  between operations  13.9 us (7%)
    ppermute x6, waiting for transfers between devices, from_behind(): return lax.ppermute(block, axis, route)  31.7 us
    all_to_all x1, waiting for transfers between devices, shards(): lax.all_to_all(outgoing, 'ctx', split_axis=0, concat_axis=0, tiled=True)  19.9 us
    ppermute x6, starting transfers between devices, from_behind(): return lax.ppermute(block, axis, route)  17.3 us
    dot_general x1, matrix products, attend(): jnp.einsum('hgrk,khd->rhgd', rounded, v_heads, preferred_element_type=jnp...  14.5 us
    dot_general x1, matrix products, attend(): jnp.einsum('rhgd,khd->hgrk', q_heads, k_heads, preferred_element_type=jnp...  13.6 us
    reduce_sum x1, other arithmetic, attend(): total = jnp.sum(weights, axis=-1)  12.8 us
    all_to_all x1, starting transfers between devices, shards(): lax.all_to_all(outgoing, 'ctx', split_axis=0, concat_axis=0, tiled=True)  12 us
    dot_general x1, matrix products, project(): jnp.dot(normed, w_query, preferred_element_type=jnp.float32)  8.18 us
  transfers between devices with their start and end apart: 7, of which 3 were waited for; matrix products, arithmetic and copies ran while one was open for 10% of the time, Pallas kernels for 0%

commit v1 on v0

v1 whole, which is shorter than its diff:
```python
import functools

import jax
import jax.numpy as jnp
import numpy as np
from jax import lax
from jax.experimental import pallas as pl
from jax.experimental.pallas import tpu as pltpu
from jax.sharding import PartitionSpec as P

HEAD = 128
BLOCK = 128
ROPE_THETA = 500000.0
EPSILON = 1e-05
MASKED = -1e30
GROUP = 4
REACH = 3 * BLOCK
RUN = GROUP * BLOCK
MESH = pl.DeviceIdType.MESH
F32 = jnp.float32
BF16 = jnp.bfloat16
I32 = jnp.int32


def iota(shape, axis):
    return lax.broadcasted_iota(I32, shape, axis)


def column_of(row):
    n = row.shape[1]
    eye = iota((n, n), 0) == iota((n, n), 1)
    return jnp.sum(jnp.where(eye, row, 0), axis=1, keepdims=True)


def row_of(column):
    n = column.shape[0]
    eye = iota((n, n), 0) == iota((n, n), 1)
    return jnp.sum(jnp.where(eye, column, 0), axis=0, keepdims=True)


def kernel(
    n,
    tokens,
    positions,
    lengths,
    gain,
    freq,
    w_query,
    w_key,
    w_value,
    out,
    x,
    normed,
    xs,
    perm,
    wbuf,
    cosine,
    sine,
    send,
    recv,
    code,
    slot,
    slot_row,
    onehot,
    kv,
    bias,
    qs,
    osend,
    tok_sem,
    w_sem,
    send_sem,
    recv_sem,
    halo_send,
    halo_recv,
    out_send,
    out_recv,
):
    groups = n // GROUP
    rows, width = tokens.shape
    per = rows // groups
    total = n * per
    me = lax.axis_index("ctx")
    mine = lax.div(me, GROUP)
    head = lax.rem(me, GROUP)

    tok_chunks = tok_sem.shape[0]
    tok_rows = rows // tok_chunks

    def tok_copy(c):
        part = pl.ds(c * tok_rows, tok_rows)
        return pltpu.make_async_copy(tokens.at[part], x.at[part], tok_sem.at[c])

    for c in range(tok_chunks):
        tok_copy(c).start()

    def head_at(i):
        return lax.rem(head + i, GROUP)

    for i in range(GROUP):
        at = pl.ds(pl.multiple_of(head_at(i) * HEAD, HEAD), HEAD)
        pltpu.make_async_copy(w_key.at[:, at], wbuf.at[i, :, pl.ds(0, HEAD)], w_sem.at[i]).start()
        pltpu.make_async_copy(w_value.at[:, at], wbuf.at[i, :, pl.ds(HEAD, HEAD)], w_sem.at[i]).start()
    for t in (1, 2):
        for i in range(GROUP):
            at = pl.ds(pl.multiple_of(head_at(i) * 4 * HEAD + (t - 1) * 2 * HEAD, 2 * HEAD), 2 * HEAD)
            k = t * GROUP + i
            pltpu.make_async_copy(w_query.at[:, at], wbuf.at[k], w_sem.at[k]).start()

    barrier = pltpu.get_barrier_semaphore()

    def greet(r, carry):
        pl.semaphore_signal(
            barrier, inc=1, device_id={"ctx": lax.rem(me + r, n)}, device_id_type=MESH
        )
        return carry

    lax.fori_loop(1, n, greet, 0)

    def group_of(where):
        block = lax.shift_right_logical(where, 7)
        return lax.shift_right_logical(jnp.minimum(block, 2 * n - 1 - block), 2)

    here = jnp.concatenate(
        [positions[pl.ds(2 * me, 1), :], positions[pl.ds(2 * me + 1, 1), :]], axis=1
    )
    group_row = group_of(here)
    group_col = column_of(group_row)
    before = (group_col == group_row) & (iota((rows, rows), 0) < iota((rows, rows), 1))
    rank = group_row * per + jnp.sum(before.astype(I32), axis=0, keepdims=True)
    chosen = iota((rows, rows), 0) == rank
    perm[...] = chosen.astype(F32).astype(BF16)
    where_at = jnp.sum(jnp.where(chosen, here, 0), axis=1, keepdims=True)
    angle = where_at.astype(F32) * freq[...]
    sign = jnp.where(iota((1, HEAD), 1) < HEAD // 2, -1.0, 1.0)
    cosine[...] = jnp.cos(angle)
    sine[...] = jnp.sin(angle) * sign

    tiles = width // HEAD
    for c in range(tok_chunks):
        tok_copy(c).wait()
        part = pl.ds(c * tok_rows, tok_rows)
        square = jnp.zeros((tok_rows, HEAD), F32)
        for j in range(tiles):
            v = x[part, pl.ds(j * HEAD, HEAD)].astype(F32)
            square = square + v * v
        mean = jnp.sum(square, axis=1, keepdims=True) * (1.0 / width)
        scale = lax.rsqrt(mean + EPSILON)
        for j in range(tiles):
            at = pl.ds(j * HEAD, HEAD)
            v = x[part, at].astype(F32) * scale * gain[:, at].astype(F32)
            normed[part, at] = v.astype(BF16)
    step = min(512, width)
    for j in range(width // step):
        at = pl.ds(j * step, step)
        xs[:, at] = jnp.dot(perm[...], normed[:, at], preferred_element_type=F32).astype(BF16)

    def message(t, i, r):
        g = lax.rem(mine + r, groups)
        return send.at[t, i, g], g * GROUP + head_at(i)

    pl.semaphore_wait(barrier, n - 1)

    for t in range(3):

        def project(i, carry, t=t):
            k = t * GROUP + i
            pltpu.make_async_copy(wbuf.at[k], wbuf.at[k], w_sem.at[k]).wait()
            got = jnp.dot(xs[...], wbuf[k], preferred_element_type=F32)
            for c in range(2):
                u = got[:, c * HEAD : (c + 1) * HEAD]
                if t > 0 or c == 0:
                    u = u * cosine[...] + pltpu.roll(u, HEAD // 2, axis=1) * sine[...]
                send[t, i, :, c] = u.astype(BF16).reshape(groups, per, HEAD)

            def post(r, carry):
                src, dest = message(t, i, r)
                pltpu.make_async_remote_copy(
                    src_ref=src,
                    dst_ref=recv.at[t, me],
                    send_sem=send_sem.at[t],
                    recv_sem=recv_sem.at[t],
                    device_id={"ctx": dest},
                    device_id_type=MESH,
                ).start()
                return carry

            lax.fori_loop(1, groups, post, 0)

            @pl.when(i > 0)
            def _():
                post(0, 0)

            @pl.when(i == 0)
            def _():
                src, _ = message(t, i, 0)
                pltpu.make_async_copy(src, recv.at[t, me], recv_sem.at[t]).start()

            return carry

        lax.fori_loop(0, GROUP, project, 0)

    low_base = mine * RUN
    high_base = (2 * n - GROUP - GROUP * mine) * BLOCK
    table = positions[...]
    tall = table.shape[0]
    member = group_of(table) == mine
    ones = member.astype(F32)
    upper = (iota((BLOCK, BLOCK), 0) < iota((BLOCK, BLOCK), 1)).astype(F32).astype(BF16)
    ahead = jnp.dot(ones.astype(BF16), upper, preferred_element_type=F32)
    count = jnp.broadcast_to(jnp.sum(ones, axis=1, keepdims=True), ones.shape)
    odd = lax.rem(iota((tall, BLOCK), 0), 2) == 1
    ahead = ahead + jnp.where(odd, pltpu.roll(count, 1, axis=0), 0.0)
    code[...] = jnp.where(member, ahead.astype(I32), -1)
    slot[...] = jnp.where(table < n * BLOCK, table - low_base, table - high_base + RUN)
    together = BLOCK // per
    kth = iota((per, BLOCK), 0)

    def place(b, carry):
        parts = []
        for q in range(together):
            s = b * together + q
            found = jnp.zeros((per, BLOCK), I32)
            for e in range(2):
                line = pl.ds(2 * s + e, 1)
                found = found + jnp.where(code[line, :] == kth, slot[line, :], 0)
            parts.append(jnp.sum(found, axis=1, keepdims=True))
        column = parts[0] if together == 1 else jnp.concatenate(parts, axis=0)
        slot_row[pl.ds(b, 1), :] = row_of(column)
        return carry

    lax.fori_loop(0, total // BLOCK, place, 0)

    def spread(b, carry):
        first = pl.multiple_of(b * BLOCK, BLOCK)
        want = iota((BLOCK, BLOCK), 0) + first
        for j in range(total // BLOCK):
            hit = want == slot_row[pl.ds(j, 1), :]
            onehot[pl.ds(first, BLOCK), pl.ds(j * BLOCK, BLOCK)] = hit.astype(F32).astype(BF16)
        return carry

    lax.fori_loop(0, total // BLOCK, spread, 0)

    length_col = column_of(lengths[...])
    docs = lengths.shape[1]
    ends = jnp.sum(
        jnp.where(iota((docs, docs), 0) <= iota((docs, docs), 1), length_col, 0), axis=0, keepdims=True
    )
    for run, base in ((0, low_base), (1, high_base)):

        def fill(b, carry, run=run, base=base):
            at = base + b * BLOCK + iota((BLOCK, 1), 0)
            start = jnp.max(jnp.where(ends <= at, ends, 0), axis=1, keepdims=True)
            key = iota((BLOCK, REACH + BLOCK), 1)
            open_ = (key <= REACH + iota((BLOCK, REACH + BLOCK), 0)) & (
                key >= start - (base + b * BLOCK - REACH)
            )
            bias[run, b] = jnp.where(open_, 0.0, MASKED)
            return carry

        lax.fori_loop(0, GROUP, fill, 0)

    def arrived(t):
        pltpu.make_async_copy(recv.at[t], recv.at[t], recv_sem.at[t]).wait()
        both = jnp.concatenate(
            [recv[t, :, c].reshape(total, HEAD) for c in range(2)], axis=1
        )
        return both

    both = arrived(0)
    for run in range(2):
        got = jnp.dot(
            onehot[pl.ds(run * RUN, RUN), :], both, preferred_element_type=F32
        ).astype(BF16)
        for c in range(2):
            kv[run, c, pl.ds(REACH, RUN), :] = got[:, c * HEAD : (c + 1) * HEAD]

    tail = pl.ds(RUN, REACH)
    lead = pl.ds(0, REACH)

    def halo(run, dest):
        return pltpu.make_async_remote_copy(
            src_ref=kv.at[run, :, tail],
            dst_ref=kv.at[run, :, lead],
            send_sem=halo_send.at[run],
            recv_sem=halo_recv.at[run],
            device_id={"ctx": dest},
            device_id_type=MESH,
        )

    last = groups - 1

    @pl.when(mine < last)
    def _():
        halo(0, me + GROUP).start()

    @pl.when(mine > 0)
    def _():
        halo(1, me - GROUP).start()

    @pl.when(mine == last)
    def _():
        pltpu.make_async_copy(kv.at[0, :, tail], kv.at[1, :, lead], halo_recv.at[1]).start()

    @pl.when(mine == 0)
    def _():
        for c in range(2):
            kv[0, c, lead, :] = jnp.zeros((REACH, HEAD), BF16)

    factor = np.float32(np.log2(np.e) / HEAD**0.5)

    def out_copy(t, owner, run):
        src = osend.at[t - 1, owner, run]
        dst = out.at[
            pl.ds(run * BLOCK, BLOCK),
            pl.ds(pl.multiple_of(head * 4 * HEAD + (t - 1) * 2 * HEAD, 2 * HEAD), 2 * HEAD),
        ]
        return src, dst

    for t in (1, 2):
        both = arrived(t)
        for run in range(2):
            got = jnp.dot(
                onehot[pl.ds(run * RUN, RUN), :], both, preferred_element_type=F32
            ).astype(BF16)
            for c in range(2):
                qs[run, c] = got[:, c * HEAD : (c + 1) * HEAD]
        if t == 1:

            @pl.when(mine > 0)
            def _():
                halo(0, me).wait_recv()

            halo(1, me).wait_recv()

        def attend(i, carry, t=t):
            owner = lax.rem(head + 1 + i, GROUP)
            for run in range(2):
                b = owner if run == 0 else GROUP - 1 - owner
                first = pl.multiple_of(b * BLOCK, BLOCK)
                key = kv[run, 0, pl.ds(first, REACH + BLOCK), :]
                value = kv[run, 1, pl.ds(first, REACH + BLOCK), :]
                query = jnp.concatenate([qs[run, c, pl.ds(first, BLOCK), :] for c in range(2)], axis=0)
                s = lax.dot_general(
                    query, key, (((1,), (1,)), ((), ())), preferred_element_type=F32
                )
                mask = bias[run, b]
                s = s + jnp.concatenate([mask, mask], axis=0)
                top = jnp.max(s, axis=1, keepdims=True)
                weights = jnp.exp2((s - top) * factor)
                mass = jnp.sum(weights, axis=1, keepdims=True)
                mixed = jnp.dot(weights.astype(BF16), value, preferred_element_type=F32)
                mixed = (mixed / mass).astype(BF16)
                for c in range(2):
                    osend[t - 1, owner, run, :, pl.ds(c * HEAD, HEAD)] = mixed[
                        c * BLOCK : (c + 1) * BLOCK
                    ]
            for run in range(2):
                src, dst = out_copy(t, owner, run)

                @pl.when(i < GROUP - 1)
                def _(src=src, dst=dst):
                    pltpu.make_async_remote_copy(
                        src_ref=src,
                        dst_ref=dst,
                        send_sem=out_send,
                        recv_sem=out_recv,
                        device_id={"ctx": mine * GROUP + owner},
                        device_id_type=MESH,
                    ).start()

                @pl.when(i == GROUP - 1)
                def _(src=src, dst=dst):
                    pltpu.make_async_copy(src, dst, out_recv).start()

            return carry

        lax.fori_loop(0, GROUP, attend, 0)

    pltpu.make_async_copy(out, out, out_recv).wait()
    sent = osend.at[:, pl.ds(0, GROUP - 1)]
    pltpu.make_async_copy(sent, sent, out_send).wait()

    @pl.when(mine < last)
    def _():
        halo(0, me).wait_send()

    @pl.when(mine > 0)
    def _():
        halo(1, me).wait_send()

    for t in range(3):
        done = recv.at[t, pl.ds(0, n - 1)]
        pltpu.make_async_copy(done, done, send_sem.at[t]).wait()


def shards(n, tokens, positions, lengths, gain, w_query, w_key, value_weight):
    rows, width = tokens.shape
    groups = n // GROUP
    per = rows // groups
    total = n * per
    half = HEAD // 2
    freq = (
        np.float32(ROPE_THETA) ** (-(np.arange(half, dtype=np.float32) * 2.0 / HEAD))
    ).astype(np.float32)
    freq = jnp.asarray(np.concatenate([freq, freq])[None])
    vmem = pl.BlockSpec(memory_space=pltpu.VMEM)
    anywhere = pl.BlockSpec(memory_space=pl.ANY)
    sem = pltpu.SemaphoreType.DMA
    return pl.pallas_call(
        functools.partial(kernel, n),
        name="attention",
        out_shape=jax.ShapeDtypeStruct((rows, w_query.shape[1]), BF16),
        in_specs=[anywhere, vmem, vmem, vmem, vmem, anywhere, anywhere, anywhere],
        out_specs=anywhere,
        scratch_shapes=[
            pltpu.VMEM((rows, width), BF16),
            pltpu.VMEM((rows, width), BF16),
            pltpu.VMEM((rows, width), BF16),
            pltpu.VMEM((rows, rows), BF16),
            pltpu.VMEM((3 * GROUP, width, 2 * HEAD), BF16),
            pltpu.VMEM((rows, HEAD), F32),
            pltpu.VMEM((rows, HEAD), F32),
            pltpu.VMEM((3, GROUP, groups, 2, per, HEAD), BF16),
            pltpu.VMEM((3, n, 2, per, HEAD), BF16),
            pltpu.VMEM((2 * n, BLOCK), I32),
            pltpu.VMEM((2 * n, BLOCK), I32),
            pltpu.VMEM((total // BLOCK, BLOCK), I32),
            pltpu.VMEM((total, total), BF16),
            pltpu.VMEM((2, 2, REACH + RUN, HEAD), BF16),
            pltpu.VMEM((2, GROUP, BLOCK, REACH + BLOCK), F32),
            pltpu.VMEM((2, 2, RUN, HEAD), BF16),
            pltpu.VMEM((2, GROUP, 2, BLOCK, 2 * HEAD), BF16),
            sem((4,)),
            sem((3 * GROUP,)),
            sem((3,)),
            sem((3,)),
            sem((2,)),
            sem((2,)),
            sem,
            sem,
        ],
        compiler_params=pltpu.CompilerParams(
            collective_id=0, has_side_effects=True, vmem_limit_bytes=60 * 1024 * 1024
        ),
    )(
        tokens,
        positions.reshape(2 * n, BLOCK),
        lengths.reshape(1, lengths.shape[0]),
        gain.reshape(1, width),
        freq,
        w_query,
        w_key,
        value_weight,
    )


def solution(mesh):
    in_specs = (P(("dp", "ctx"), None), P("dp"), P("dp"), P(), P(), P(), P())
    out_specs = P(("dp", "ctx"), None)
    return jax.shard_map(
        functools.partial(shards, mesh.shape["ctx"]),
        mesh=mesh,
        in_specs=in_specs,
        out_specs=out_specs,
        check_vma=False,
    )
```

time: 200 us -> 56.6 us (0.28)
  the two profiles are of different devices: /device:TPU:0 before, /device:TPU:38 now
where the time goes in v1:
time: 56.6 us; the launch traced here: 56.4 us
  Pallas kernels  52.8 us (93%)
  local copies, waits for them, and re-layouts  3.62 us (6%)
    pallas_call x1, Pallas kernels, shards(): pl.pallas_call(functools.partial(kernel, n), name='attention', out_shape=...  52.8 us
    unnamed x1, local copies, waits for them, and re-layouts  2.3 us
    reshape x1, local copies, waits for them, and re-layouts, shards(): gain.reshape(1, width)  1.31 us

profile of v1, /device:TPU:38, one launch (start us, length us, event | category | flops | bytes accessed | tf_op | source)
XLA Modules:
  0.0 56.4 jit_solution(4173589811305493715)
XLA Ops:
  0.0 1.3 %reshape.11.gain = bf16[1,4096]{1,0:T(2,128)(2,1)} reshape(bf16[4096]{0:T(1024)(128)(2,1)} %param.11) | data formatting | bytes 16384 | tf_op jit(solution)/shard_map/reshape | solution.py:449
  1.3 52.8 %attention.1 = bf16[256,2048]{1,0:T(8,128)(2,1)} custom-call(bf16[256,4096]{1,0:T(8,128)(2,1)} %tokens.1, s32[128,128]{1,0:T(8,128)} %bitcast.2, s32[1,128]{1,0:T(1,128)} %bitcast.3, bf16[1,4096]{1,0:T(2,128)(2,1)} %reshape.11.gain, f32[1,128]{1,0:T(1,128)} %constant.2.clone.freq, bf16[4096,2048]{1,0:T(8,128)(2,1)} %w_query.1, bf16[4096,512]{1,0:T(8,128)(2,1)} %w_key.1, ...), custom_call_target="tpu_custom_call" | custom-call | tf_op jit(solution)/shard_map/attention/pallas_call | solution.py:409
  54.1 2.3 %copy.10 = bf16[256,2048]{1,0:T(8,128)(2,1)} copy(bf16[256,2048]{1,0:T(8,128)(2,1)} %attention.1) | data formatting | bytes 2097152

commit v2 on v1

--- a/solution.py
+++ b/solution.py
@@ -14,6 +14,7 @@
 EPSILON = 1e-05
 MASKED = -1e30
 GROUP = 4
+AHEAD = 2
 REACH = 3 * BLOCK
 RUN = GROUP * BLOCK
 MESH = pl.DeviceIdType.MESH
@@ -96,15 +97,23 @@
     def head_at(i):
         return lax.rem(head + i, GROUP)
 
-    for i in range(GROUP):
-        at = pl.ds(pl.multiple_of(head_at(i) * HEAD, HEAD), HEAD)
-        pltpu.make_async_copy(w_key.at[:, at], wbuf.at[i, :, pl.ds(0, HEAD)], w_sem.at[i]).start()
-        pltpu.make_async_copy(w_value.at[:, at], wbuf.at[i, :, pl.ds(HEAD, HEAD)], w_sem.at[i]).start()
-    for t in (1, 2):
-        for i in range(GROUP):
-            at = pl.ds(pl.multiple_of(head_at(i) * 4 * HEAD + (t - 1) * 2 * HEAD, 2 * HEAD), 2 * HEAD)
-            k = t * GROUP + i
-            pltpu.make_async_copy(w_query.at[:, at], wbuf.at[k], w_sem.at[k]).start()
+    def fetch(k):
+        t, i = divmod(k, GROUP)
+        if t == 0:
+            at = pl.ds(pl.multiple_of(head_at(i) * HEAD, HEAD), HEAD)
+            return [
+                pltpu.make_async_copy(w.at[:, at], wbuf.at[k, :, pl.ds(c * HEAD, HEAD)], w_sem.at[k])
+                for c, w in enumerate((w_key, w_value))
+            ]
+        at = pl.ds(pl.multiple_of(head_at(i) * 4 * HEAD + (t - 1) * 2 * HEAD, 2 * HEAD), 2 * HEAD)
+        return [pltpu.make_async_copy(w_query.at[:, at], wbuf.at[k], w_sem.at[k])]
+
+    def start(k):
+        for copy in fetch(k):
+            copy.start()
+
+    for k in range(AHEAD):
+        start(k)
 
     barrier = pltpu.get_barrier_semaphore()
 
@@ -136,6 +145,7 @@
     sine[...] = jnp.sin(angle) * sign
 
     tiles = width // HEAD
+    gains = gain[...].astype(F32)
     for c in range(tok_chunks):
         tok_copy(c).wait()
         part = pl.ds(c * tok_rows, tok_rows)
@@ -147,7 +157,7 @@
         scale = lax.rsqrt(mean + EPSILON)
         for j in range(tiles):
             at = pl.ds(j * HEAD, HEAD)
-            v = x[part, at].astype(F32) * scale * gain[:, at].astype(F32)
+            v = x[part, at].astype(F32) * scale * gains[j : j + 1]
             normed[part, at] = v.astype(BF16)
     step = min(512, width)
     for j in range(width // step):
@@ -158,46 +168,44 @@
         g = lax.rem(mine + r, groups)
         return send.at[t, i, g], g * GROUP + head_at(i)
 
-    pl.semaphore_wait(barrier, n - 1)
+    def dispatch(t, i):
+        def post(r, carry):
+            src, dest = message(t, i, r)
+            pltpu.make_async_remote_copy(
+                src_ref=src,
+                dst_ref=recv.at[t, me],
+                send_sem=send_sem.at[t],
+                recv_sem=recv_sem.at[t],
+                device_id={"ctx": dest},
+                device_id_type=MESH,
+            ).start()
+            return carry
+
+        lax.fori_loop(1, groups, post, 0)
+        if i > 0:
+            post(0, 0)
+        else:
+            src, _ = message(t, i, 0)
+            pltpu.make_async_copy(src, recv.at[t, me], recv_sem.at[t]).start()
 
     for t in range(3):
-
-        def project(i, carry, t=t):
+        for i in range(GROUP):
             k = t * GROUP + i
             pltpu.make_async_copy(wbuf.at[k], wbuf.at[k], w_sem.at[k]).wait()
+            if k + AHEAD < 3 * GROUP:
+                start(k + AHEAD)
             got = jnp.dot(xs[...], wbuf[k], preferred_element_type=F32)
             for c in range(2):
                 u = got[:, c * HEAD : (c + 1) * HEAD]
                 if t > 0 or c == 0:
                     u = u * cosine[...] + pltpu.roll(u, HEAD // 2, axis=1) * sine[...]
                 send[t, i, :, c] = u.astype(BF16).reshape(groups, per, HEAD)
-
-            def post(r, carry):
-                src, dest = message(t, i, r)
-                pltpu.make_async_remote_copy(
-                    src_ref=src,
-                    dst_ref=recv.at[t, me],
-                    send_sem=send_sem.at[t],
-                    recv_sem=recv_sem.at[t],
-                    device_id={"ctx": dest},
-                    device_id_type=MESH,
-                ).start()
-                return carry
-
-            lax.fori_loop(1, groups, post, 0)
-
-            @pl.when(i > 0)
-            def _():
-                post(0, 0)
-
-            @pl.when(i == 0)
-            def _():
-                src, _ = message(t, i, 0)
-                pltpu.make_async_copy(src, recv.at[t, me], recv_sem.at[t]).start()
-
-            return carry
-
-        lax.fori_loop(0, GROUP, project, 0)
+            if k == GROUP - 1:
+                pl.semaphore_wait(barrier, n - 1)
+                for j in range(k):
+                    dispatch(0, j)
+            if k >= GROUP - 1:
+                dispatch(t, i)
 
     low_base = mine * RUN
     high_base = (2 * n - GROUP - GROUP * mine) * BLOCK
@@ -409,9 +417,9 @@
     return pl.pallas_call(
         functools.partial(kernel, n),
         name="attention",
-        out_shape=jax.ShapeDtypeStruct((rows, w_query.shape[1]), BF16),
+        out_shape=pltpu.VMEM((rows, w_query.shape[1]), BF16),
         in_specs=[anywhere, vmem, vmem, vmem, vmem, anywhere, anywhere, anywhere],
-        out_specs=anywhere,
+        out_specs=vmem,
         scratch_shapes=[
             pltpu.VMEM((rows, width), BF16),
             pltpu.VMEM((rows, width), BF16),
@@ -446,7 +454,7 @@
         tokens,
         positions.reshape(2 * n, BLOCK),
         lengths.reshape(1, lengths.shape[0]),
-        gain.reshape(1, width),
+        gain.reshape(width // HEAD, HEAD),
         freq,
         w_query,
         w_key,

time: 56.6 us -> 51.7 us (0.913)
  the two profiles are of different devices: /device:TPU:38 before, /device:TPU:105 now
where the time goes in v2:
time: 51.7 us; the launch traced here: 51.5 us
  Pallas kernels  50.5 us (98%)
  local copies, waits for them, and re-layouts  0.97 us (2%)
    pallas_call x1, Pallas kernels, shards(): pl.pallas_call(functools.partial(kernel, n), name='attention', out_shape=...  50.5 us

profile of v2, /device:TPU:105, one launch (start us, length us, event | category | flops | bytes accessed | tf_op | source)
XLA Modules:
  0.0 51.5 jit_solution(5704938088811123850)
XLA Ops:
  0.0 50.5 %attention.1 = bf16[256,2048]{1,0:T(8,128)(2,1)S(1)} custom-call(bf16[256,4096]{1,0:T(8,128)(2,1)} %tokens.1, s32[128,128]{1,0:T(8,128)} %bitcast.3, s32[1,128]{1,0:T(1,128)} %bitcast.5, bf16[32,128]{1,0:T(8,128)(2,1)} %bitcast.4, f32[1,128]{1,0:T(1,128)} %constant.2.clone.freq, bf16[4096,2048]{1,0:T(8,128)(2,1)} %w_query.1, bf16[4096,512]{1,0:T(8,128)(2,1)} %w_key.1, ...), custom_call_target="tpu_custom_call" | custom-call | tf_op jit(solution)/shard_map/attention/pallas_call | solution.py:417
  50.6 1.0 %copy.10 = bf16[256,2048]{1,0:T(8,128)(2,1)} copy(bf16[256,2048]{1,0:T(8,128)(2,1)S(1)} %attention.1) | data formatting | bytes 2097152

commit v3 on v2

--- a/solution.py
+++ b/solution.py
@@ -15,6 +15,7 @@
 MASKED = -1e30
 GROUP = 4
 AHEAD = 2
+HELD = 2
 REACH = 3 * BLOCK
 RUN = GROUP * BLOCK
 MESH = pl.DeviceIdType.MESH
@@ -188,6 +189,49 @@
             src, _ = message(t, i, 0)
             pltpu.make_async_copy(src, recv.at[t, me], recv_sem.at[t]).start()
 
+    low_base = mine * RUN
+    high_base = (2 * n - GROUP - GROUP * mine) * BLOCK
+
+    def arrange():
+        table = positions[...]
+        tall = table.shape[0]
+        member = group_of(table) == mine
+        ones = member.astype(F32)
+        upper = (iota((BLOCK, BLOCK), 0) < iota((BLOCK, BLOCK), 1)).astype(F32).astype(BF16)
+        ahead = jnp.dot(ones.astype(BF16), upper, preferred_element_type=F32)
+        count = jnp.broadcast_to(jnp.sum(ones, axis=1, keepdims=True), ones.shape)
+        odd = lax.rem(iota((tall, BLOCK), 0), 2) == 1
+        ahead = ahead + jnp.where(odd, pltpu.roll(count, 1, axis=0), 0.0)
+        code[...] = jnp.where(member, ahead.astype(I32), -1)
+        slot[...] = jnp.where(table < n * BLOCK, table - low_base, table - high_base + RUN)
+        together = BLOCK // per
+        kth = iota((per, BLOCK), 0)
+        for b in range(total // BLOCK):
+            parts = []
+            for q in range(together):
+                found = jnp.zeros((per, BLOCK), I32)
+                for e in range(2):
+                    line = pl.ds(2 * (b * together + q) + e, 1)
+                    found = found + jnp.where(code[line, :] == kth, slot[line, :], 0)
+                parts.append(jnp.sum(found, axis=1, keepdims=True))
+            column = parts[0] if together == 1 else jnp.concatenate(parts, axis=0)
+            slot_row[pl.ds(b, 1), :] = row_of(column)
+        lines = iota((BLOCK, BLOCK), 0).astype(F32).astype(BF16)
+
+        def spread(b, carry):
+            first = pl.multiple_of(b * BLOCK, BLOCK)
+            for j in range(total // BLOCK):
+                want = slot_row[pl.ds(j, 1), :] - first
+                want = jnp.where((want >= 0) & (want < BLOCK), want, -1)
+                want = jnp.broadcast_to(want, (16, BLOCK)).astype(F32).astype(BF16)
+                hit = lines == jnp.concatenate([want] * (BLOCK // 16), axis=0)
+                onehot[pl.ds(first, BLOCK), pl.ds(j * BLOCK, BLOCK)] = jnp.where(
+                    hit, jnp.ones((), BF16), jnp.zeros((), BF16)
+                )
+            return carry
+
+        lax.fori_loop(0, total // BLOCK, spread, 0)
+
     for t in range(3):
         for i in range(GROUP):
             k = t * GROUP + i
@@ -204,49 +248,60 @@
                 pl.semaphore_wait(barrier, n - 1)
                 for j in range(k):
                     dispatch(0, j)
-            if k >= GROUP - 1:
+            if k >= GROUP - 1 and k < 3 * GROUP - HELD:
                 dispatch(t, i)
-
-    low_base = mine * RUN
-    high_base = (2 * n - GROUP - GROUP * mine) * BLOCK
-    table = positions[...]
-    tall = table.shape[0]
-    member = group_of(table) == mine
-    ones = member.astype(F32)
-    upper = (iota((BLOCK, BLOCK), 0) < iota((BLOCK, BLOCK), 1)).astype(F32).astype(BF16)
-    ahead = jnp.dot(ones.astype(BF16), upper, preferred_element_type=F32)
-    count = jnp.broadcast_to(jnp.sum(ones, axis=1, keepdims=True), ones.shape)
-    odd = lax.rem(iota((tall, BLOCK), 0), 2) == 1
-    ahead = ahead + jnp.where(odd, pltpu.roll(count, 1, axis=0), 0.0)
-    code[...] = jnp.where(member, ahead.astype(I32), -1)
-    slot[...] = jnp.where(table < n * BLOCK, table - low_base, table - high_base + RUN)
-    together = BLOCK // per
-    kth = iota((per, BLOCK), 0)
-
-    def place(b, carry):
-        parts = []
-        for q in range(together):
-            s = b * together + q
-            found = jnp.zeros((per, BLOCK), I32)
-            for e in range(2):
-                line = pl.ds(2 * s + e, 1)
-                found = found + jnp.where(code[line, :] == kth, slot[line, :], 0)
-            parts.append(jnp.sum(found, axis=1, keepdims=True))
-        column = parts[0] if together == 1 else jnp.concatenate(parts, axis=0)
-        slot_row[pl.ds(b, 1), :] = row_of(column)
-        return carry
-
-    lax.fori_loop(0, total // BLOCK, place, 0)
-
-    def spread(b, carry):
-        first = pl.multiple_of(b * BLOCK, BLOCK)
-        want = iota((BLOCK, BLOCK), 0) + first
-        for j in range(total // BLOCK):
-            hit = want == slot_row[pl.ds(j, 1), :]
-            onehot[pl.ds(first, BLOCK), pl.ds(j * BLOCK, BLOCK)] = hit.astype(F32).astype(BF16)
-        return carry
-
-    lax.fori_loop(0, total // BLOCK, spread, 0)
+            if k == GROUP - 1:
+                arrange()
+
+    def arrived(t):
+        pltpu.make_async_copy(recv.at[t], recv.at[t], recv_sem.at[t]).wait()
+        both = jnp.concatenate(
+            [recv[t, :, c].reshape(total, HEAD) for c in range(2)], axis=1
+        )
+        return both
+
+    both = arrived(0)
+    for run in range(2):
+        got = jnp.dot(
+            onehot[pl.ds(run * RUN, RUN), :], both, preferred_element_type=F32
+        ).astype(BF16)
+        for c in range(2):
+            kv[run, c, pl.ds(REACH, RUN), :] = got[:, c * HEAD : (c + 1) * HEAD]
+
+    tail = pl.ds(RUN, REACH)
+    lead = pl.ds(0, REACH)
+
+    def halo(run, dest):
+        return pltpu.make_async_remote_copy(
+            src_ref=kv.at[run, :, tail],
+            dst_ref=kv.at[run, :, lead],
+            send_sem=halo_send.at[run],
+            recv_sem=halo_recv.at[run],
+            device_id={"ctx": dest},
+            device_id_type=MESH,
+        )
+
+    last = groups - 1
+
+    @pl.when(mine < last)
+    def _():
+        halo(0, me + GROUP).start()
+
+    @pl.when(mine > 0)
+    def _():
+        halo(1, me - GROUP).start()
+
+    @pl.when(mine == last)
+    def _():
+        pltpu.make_async_copy(kv.at[0, :, tail], kv.at[1, :, lead], halo_recv.at[1]).start()
+
+    @pl.when(mine == 0)
+    def _():
+        for c in range(2):
+            kv[0, c, lead, :] = jnp.zeros((REACH, HEAD), BF16)
+
+    for i in range(GROUP - HELD, GROUP):
+        dispatch(2, i)
 
     length_col = column_of(lengths[...])
     docs = lengths.shape[1]
@@ -266,53 +321,6 @@
             return carry
 
         lax.fori_loop(0, GROUP, fill, 0)
-
-    def arrived(t):
-        pltpu.make_async_copy(recv.at[t], recv.at[t], recv_sem.at[t]).wait()
-        both = jnp.concatenate(
-            [recv[t, :, c].reshape(total, HEAD) for c in range(2)], axis=1
-        )
-        return both
-
-    both = arrived(0)
-    for run in range(2):
-        got = jnp.dot(
-            onehot[pl.ds(run * RUN, RUN), :], both, preferred_element_type=F32
-        ).astype(BF16)
-        for c in range(2):
-            kv[run, c, pl.ds(REACH, RUN), :] = got[:, c * HEAD : (c + 1) * HEAD]
-
-    tail = pl.ds(RUN, REACH)
-    lead = pl.ds(0, REACH)
-
-    def halo(run, dest):
-        return pltpu.make_async_remote_copy(
-            src_ref=kv.at[run, :, tail],
-            dst_ref=kv.at[run, :, lead],
-            send_sem=halo_send.at[run],
-            recv_sem=halo_recv.at[run],
-            device_id={"ctx": dest},
-            device_id_type=MESH,
-        )
-
-    last = groups - 1
-
-    @pl.when(mine < last)
-    def _():
-        halo(0, me + GROUP).start()
-
-    @pl.when(mine > 0)
-    def _():
-        halo(1, me - GROUP).start()
-
-    @pl.when(mine == last)
-    def _():
-        pltpu.make_async_copy(kv.at[0, :, tail], kv.at[1, :, lead], halo_recv.at[1]).start()
-
-    @pl.when(mine == 0)
-    def _():
-        for c in range(2):
-            kv[0, c, lead, :] = jnp.zeros((REACH, HEAD), BF16)
 
     factor = np.float32(np.log2(np.e) / HEAD**0.5)
 

time: 51.7 us -> 50.2 us (0.971)
  the two profiles are of different devices: /device:TPU:105 before, /device:TPU:0 now
where the time goes in v3:
time: 50.2 us; the launch traced here: 50 us
  Pallas kernels  49.1 us (98%)
  local copies, waits for them, and re-layouts  0.97 us (2%)
    pallas_call x1, Pallas kernels, shards(): pl.pallas_call(functools.partial(kernel, n), name='attention', out_shape=...  49.1 us

profile of v3, /device:TPU:0, one launch (start us, length us, event | category | flops | bytes accessed | tf_op | source)
XLA Modules:
  0.0 50.0 jit_solution(7938540293157620979)
XLA Ops:
  0.0 49.1 %attention.1 = bf16[256,2048]{1,0:T(8,128)(2,1)S(1)} custom-call(bf16[256,4096]{1,0:T(8,128)(2,1)} %tokens.1, s32[128,128]{1,0:T(8,128)} %bitcast.3, s32[1,128]{1,0:T(1,128)} %bitcast.5, bf16[32,128]{1,0:T(8,128)(2,1)} %bitcast.4, f32[1,128]{1,0:T(1,128)} %constant.2.clone.freq, bf16[4096,2048]{1,0:T(8,128)(2,1)} %w_query.1, bf16[4096,512]{1,0:T(8,128)(2,1)} %w_key.1, ...), custom_call_target="tpu_custom_call" | custom-call | tf_op jit(solution)/shard_map/attention/pallas_call | solution.py:425
  49.1 1.0 %copy.10 = bf16[256,2048]{1,0:T(8,128)(2,1)} copy(bf16[256,2048]{1,0:T(8,128)(2,1)S(1)} %attention.1) | data formatting | bytes 2097152

commit v4 on v3

--- a/solution.py
+++ b/solution.py
@@ -16,6 +16,7 @@
 GROUP = 4
 AHEAD = 2
 HELD = 2
+TURNS = (0, 2, 1, 3)
 REACH = 3 * BLOCK
 RUN = GROUP * BLOCK
 MESH = pl.DeviceIdType.MESH
@@ -96,7 +97,7 @@
         tok_copy(c).start()
 
     def head_at(i):
-        return lax.rem(head + i, GROUP)
+        return lax.rem(head + TURNS[i], GROUP)
 
     def fetch(k):
         t, i = divmod(k, GROUP)

time: 50.2 us -> 49.8 us (level)
  no operation moved by 1% of the time
where the time goes in v4:
time: 49.8 us; the launch traced here: 49.7 us
  Pallas kernels  48.7 us (98%)
  local copies, waits for them, and re-layouts  0.97 us (2%)
    pallas_call x1, Pallas kernels, shards(): pl.pallas_call(functools.partial(kernel, n), name='attention', out_shape=...  48.7 us

profile of v4, /device:TPU:0, one launch (start us, length us, event | category | flops | bytes accessed | tf_op | source)
XLA Modules:
  0.0 49.7 jit_solution(3199091566804129910)
XLA Ops:
  0.0 48.7 %attention.1 = bf16[256,2048]{1,0:T(8,128)(2,1)S(1)} custom-call(bf16[256,4096]{1,0:T(8,128)(2,1)} %tokens.1, s32[128,128]{1,0:T(8,128)} %bitcast.3, s32[1,128]{1,0:T(1,128)} %bitcast.5, bf16[32,128]{1,0:T(8,128)(2,1)} %bitcast.4, f32[1,128]{1,0:T(1,128)} %constant.2.clone.freq, bf16[4096,2048]{1,0:T(8,128)(2,1)} %w_query.1, bf16[4096,512]{1,0:T(8,128)(2,1)} %w_key.1, ...), custom_call_target="tpu_custom_call" | custom-call | tf_op jit(solution)/shard_map/attention/pallas_call | solution.py:426
  48.7 1.0 %copy.10 = bf16[256,2048]{1,0:T(8,128)(2,1)} copy(bf16[256,2048]{1,0:T(8,128)(2,1)S(1)} %attention.1) | data formatting | bytes 2097152

commit v5 on v4

--- a/solution.py
+++ b/solution.py
@@ -16,6 +16,8 @@
 GROUP = 4
 AHEAD = 2
 HELD = 2
+HALO_ROWS = 64
+OUT_ROWS = 32
 TURNS = (0, 2, 1, 3)
 REACH = 3 * BLOCK
 RUN = GROUP * BLOCK
@@ -282,15 +284,27 @@
             device_id_type=MESH,
         )
 
+    def halo_start(run, dest):
+        for c in range(2):
+            for j in range(REACH // HALO_ROWS):
+                pltpu.make_async_remote_copy(
+                    src_ref=kv.at[run, c, pl.ds(RUN + j * HALO_ROWS, HALO_ROWS)],
+                    dst_ref=kv.at[run, c, pl.ds(j * HALO_ROWS, HALO_ROWS)],
+                    send_sem=halo_send.at[run],
+                    recv_sem=halo_recv.at[run],
+                    device_id={"ctx": dest},
+                    device_id_type=MESH,
+                ).start()
+
     last = groups - 1
 
     @pl.when(mine < last)
     def _():
-        halo(0, me + GROUP).start()
+        halo_start(0, me + GROUP)
 
     @pl.when(mine > 0)
     def _():
-        halo(1, me - GROUP).start()
+        halo_start(1, me - GROUP)
 
     @pl.when(mine == last)
     def _():
@@ -376,14 +390,16 @@
 
                 @pl.when(i < GROUP - 1)
                 def _(src=src, dst=dst):
-                    pltpu.make_async_remote_copy(
-                        src_ref=src,
-                        dst_ref=dst,
-                        send_sem=out_send,
-                        recv_sem=out_recv,
-                        device_id={"ctx": mine * GROUP + owner},
-                        device_id_type=MESH,
-                    ).start()
+                    for j in range(BLOCK // OUT_ROWS):
+                        piece = pl.ds(j * OUT_ROWS, OUT_ROWS)
+                        pltpu.make_async_remote_copy(
+                            src_ref=src.at[piece],
+                            dst_ref=dst.at[piece],
+                            send_sem=out_send,
+                            recv_sem=out_recv,
+                            device_id={"ctx": mine * GROUP + owner},
+                            device_id_type=MESH,
+                        ).start()
 
                 @pl.when(i == GROUP - 1)
                 def _(src=src, dst=dst):

time: 49.8 us -> 49.9 us (level)
  no operation moved by 1% of the time
where the time goes in v5:
time: 49.9 us; the launch traced here: 49.7 us
  Pallas kernels  48.7 us (98%)
  local copies, waits for them, and re-layouts  0.97 us (2%)
    pallas_call x1, Pallas kernels, shards(): pl.pallas_call(functools.partial(kernel, n), name='attention', out_shape=...  48.7 us

profile of v5, /device:TPU:0, one launch (start us, length us, event | category | flops | bytes accessed | tf_op | source)
XLA Modules:
  0.0 49.7 jit_solution(14664589208135396383)
XLA Ops:
  0.0 48.7 %attention.1 = bf16[256,2048]{1,0:T(8,128)(2,1)S(1)} custom-call(bf16[256,4096]{1,0:T(8,128)(2,1)} %tokens.1, s32[128,128]{1,0:T(8,128)} %bitcast.3, s32[1,128]{1,0:T(1,128)} %bitcast.5, bf16[32,128]{1,0:T(8,128)(2,1)} %bitcast.4, f32[1,128]{1,0:T(1,128)} %constant.2.clone.freq, bf16[4096,2048]{1,0:T(8,128)(2,1)} %w_query.1, bf16[4096,512]{1,0:T(8,128)(2,1)} %w_key.1, ...), custom_call_target="tpu_custom_call" | custom-call | tf_op jit(solution)/shard_map/attention/pallas_call | solution.py:442
  48.7 1.0 %copy.10 = bf16[256,2048]{1,0:T(8,128)(2,1)} copy(bf16[256,2048]{1,0:T(8,128)(2,1)S(1)} %attention.1) | data formatting | bytes 2097152
